TPU v7x, 32 devices: a whole 2x2x4 slice. The times are simulated.
32 devices in a mesh: grp: 4 (over z), sep: 8 (over y, x, core).
Axes of the slice: x: 2, y: 2, z: 4, core: 2. Of those that a mesh axis runs over, the one named last changes fastest.
Arguments:
- tiles: bfloat16 [4, 256, 64, 128], P('grp', 'sep'), may hold values from 0.0099487305 to 0.29882812
- tile_front: int32 [4, 256, 1], P('grp', 'sep'), may hold values from 0 to 7; in each aligned block of 32 rows (0 to 31, 32 to 63, ..., all dimensions but the last counted through in order) at most 8 rows name the same one
- tile_pos: int32 [4, 256], P('grp', 'sep'), may hold values from 0 to 29
- front_slot: int32 [4, 8], P('grp'), may hold values from 0 to 7, as said below
- front_parent: int32 [4, 8], P('grp'), may hold values from 0 to 7, as said below
- pivot: float32 [4, 8, 640], P('grp'), may hold values from 4 to 40
Outputs:
- factor: float32 [4, 8, 640, 512], P('grp', 'sep')
- sep_schur: float32 [8, 128, 128], P('sep')
Inputs may be any that keep to these rules, and one draw needn't show every extreme that they name: `tile_front`: at most 8 of the tiles held by one device belong to one front. `front_slot`: each group's row is a permutation of 0 to 7. (front_parent[g, f] - front_slot[g, f]) modulo 8 is one of 0, 1, 7 and 4; in every group each of these four occurs.
All inputs are finite; a program needn't handle non-finite values.
Results may differ from a plain program's by a relative error of at most 0.0003.
Values may be sent and summed in bfloat16 or wider, within the bound.
A program may use at most 64 MiB of HBM per device.

v0:
```python
import jax
import jax.numpy as jnp
import numpy as np
from jax import lax
from jax.sharding import PartitionSpec as P

POS = 30


def passed_along(shard, axis, by):
    devices = lax.axis_size(axis)
    return lax.ppermute(shard, axis, [(i, (i + by) % devices) for i in range(devices)])


def tile_arrangement(rows, column_indices):
    row_count = 5 * column_indices // rows
    position = np.zeros((row_count, 5), np.int32)
    present = np.zeros((row_count, 5), np.float32)
    number = 0
    for row_block in range(row_count):
        for col_block in range(row_block * rows // column_indices + 1):
            position[row_block, col_block] = number
            present[row_block, col_block] = 1.0
            number += 1
    return (position, present)


def front_factor(summed, pivots, rows, column_indices):
    position, present = tile_arrangement(rows, column_indices)
    order = 5 * column_indices
    elimination_count = 4 * column_indices
    blocks = summed[position] * jnp.asarray(present, jnp.float32)[:, :, None, None]
    full = blocks.transpose(0, 2, 1, 3).reshape(order, order)
    mixed = 0.5 * (full + full.T) * (1.0 - jnp.eye(order, dtype=jnp.float32))
    front_matrix = jnp.diag(pivots + jnp.sum(mixed, 1)) - mixed
    lower_triangle = jnp.linalg.cholesky(front_matrix[:elimination_count, :elimination_count])
    under_diagonal = jax.scipy.linalg.solve_triangular(
        lower_triangle, front_matrix[elimination_count:, :elimination_count].T, lower=True
    ).T
    schur = jnp.dot(under_diagonal, under_diagonal.T, precision=lax.Precision.HIGHEST)
    return (jnp.concatenate([lower_triangle, under_diagonal], 0), schur)


def body(tiles, tile_front, tile_pos, front_slot, front_parent, pivot):
    width = lax.axis_size("sep")
    myself = lax.axis_index("sep")
    held = tiles.shape[1]
    rows = tiles.shape[2]
    column_indices = tiles.shape[3]
    fronts = front_slot.shape[1]
    room = max(2, -(-2 * held // width))
    slots = front_slot[0]
    parents = front_parent[0]
    front_ids = jnp.arange(fronts, dtype=jnp.int32)
    owner_of = jnp.sum(jnp.where(tile_front[0] == front_ids[None, :], slots[None, :], 0), 1)
    target = (owner_of[:, None] == jnp.arange(width, dtype=jnp.int32)[None, :]).astype(jnp.int32)
    rank = jnp.sum(target * (jnp.cumsum(target, 0) - 1), 1)
    place = owner_of * room + rank
    outgoing = jnp.zeros((width * room, rows, column_indices), jnp.bfloat16).at[place].set(tiles[0])
    labels = jnp.full((width * room,), -1, jnp.int32).at[place].set(tile_pos[0])
    arrived, received_position = (
        lax.all_to_all(
            outgoing.reshape(width, room, rows, column_indices),
            "sep",
            split_axis=0,
            concat_axis=0,
            tiled=True,
        ),
        lax.all_to_all(labels.reshape(width, room), "sep", split_axis=0, concat_axis=0, tiled=True),
    )
    arrived = arrived.reshape(width * room, rows, column_indices)
    received_position = received_position.reshape(width * room)
    selector = (received_position[None, :] == jnp.arange(POS, dtype=jnp.int32)[:, None]).astype(
        jnp.bfloat16
    )
    summed = jnp.einsum("ps,sij->pij", selector, arrived, preferred_element_type=jnp.float32)
    mine = slots == myself
    pivots = jnp.sum(jnp.where(mine[:, None], pivot[0], 0.0), 0)
    parent = jnp.sum(jnp.where(mine, parents, 0))
    factor, schur = front_factor(summed, pivots, rows, column_indices)
    distance = (parent - myself) % width
    local_sum = jnp.where(distance == 0, schur, 0.0)[None]
    for offset in (1, -1, width // 2):
        piece = jnp.where(distance == offset % width, schur, 0.0)[None]
        local_sum = local_sum + passed_along(piece, "sep", offset)
    total = lax.psum(local_sum, "grp")
    return (factor[None, None], total)


def solution(mesh):
    placed = (
        P("grp", "sep", None, None),
        P("grp", "sep", None),
        P("grp", "sep"),
        P("grp", None),
        P("grp", None),
        P("grp", None, None),
    )
    return jax.shard_map(
        body,
        mesh=mesh,
        in_specs=placed,
        out_specs=(P("grp", "sep", None, None), P("sep", None, None)),
        check_vma=False,
    )
```

profile of v0, /device:TPU:0, one launch (start us, length us, event | category | flops | bytes accessed | tf_op | source)
XLA Modules:
  0.0 244.2 jit_solution(3018031008141978505)
XLA Ops:
  7.2 0.9 select_reduce_fusion.5
  8.3 0.8 scatter_custom_fusion
  9.2 0.7 all_to_all.9
  9.8 5.2 %all-to-all-start = ((s32[8,1,8]{2,1,0:T(1,128)}), s32[8,1,8]{2,1,0:T(1,128)S(1)}, u32[]{:S(2)}, u32[]{:S(2)}) async-start(s32[8,1,8]{2,1,0:T(1,128)} %bitcast.6), calls=%async_computation | async-start | bytes 8192 | tf_op jit(solution)/shard_map/all_to_all | solution.py:69
  15.3 3.4 %scatter_fusion = bf16[64,64,128]{2,1,0:T(8,128)(2,1)S(1)} fusion(bf16[64,64,128]{2,1,0:T(8,128)(2,1)S(1)} %broadcast_in_dim.90, s32[32]{0:T(128)S(1)} %fusion.44, bf16[32,64,128]{2,1,0:T(8,128)(2,1)} %bitcast.120), kind=kCustom, calls=%fused_computation.2 | custom fusion | bytes 1572992 | tf_op jit(solution)/shard_map/scatter | solution.py:59
  18.7 1.7 copy.28
  20.4 4.2 %all-to-all-start.1 = ((bf16[8,8,64,128]{3,1,2,0:T(8,128)(2,1)}), bf16[8,8,64,128]{3,1,2,0:T(8,128)(2,1)S(1)}, u32[]{:S(2)}, u32[]{:S(2)}) async-start(bf16[8,8,64,128]{3,1,2,0:T(8,128)(2,1)} %copy.28), calls=%async_computation.1 | async-start | bytes 2097152 | tf_op jit(solution)/shard_map/all_to_all | solution.py:62
  24.7 0.6 fusion.45
  26.1 0.5 broadcast.253
  26.6 0.7 reduce.27
  27.4 12.6 %all-to-all-done.1 = bf16[8,8,64,128]{3,1,2,0:T(8,128)(2,1)S(1)} async-done(((bf16[8,8,64,128]{3,1,2,0:T(8,128)(2,1)}), bf16[8,8,64,128]{3,1,2,0:T(8,128)(2,1)S(1)}, u32[]{:S(2)}, u32[]{:S(2)}) %all-to-all-start.1) | async-done | bytes 1048608 | tf_op jit(solution)/shard_map/all_to_all | solution.py:62
  40.0 0.3 fusion.3
  40.3 0.6 copy.30
  40.9 0.7 gather_fusion
  41.7 1.0 copy.31
  42.7 1.6 copy.49
  44.3 2.7 %copy.32 = f32[640,640]{0,1:T(8,128)} copy(f32[640,640]{1,0:T(8,128)} %bitcast.118) | data formatting | bytes 3276800 | tf_op jit(solution)/shard_map/reshape | solution.py:33
  47.0 2.0 fusion.7
  49.0 0.5 select_subtract_fusion
  49.5 1.3 slice.135
  50.8 0.2 copy-done.1
  51.1 1.7 copy.33
  53.0 1.0 copy-done.3
  54.0 11.7 %cholesky.104 = f32[128,128]{1,0:T(8,128)S(1)} custom-call(f32[128,128]{1,0:T(8,128)S(1)} %cholesky.266), custom_call_target="Cholesky" | custom-call | tf_op jit(solution)/shard_map/jit(cholesky)/cholesky | solution.py:36
  65.7 9.8 %custom-call.31 = f32[1,128,128]{1,2,0:T(8,128)S(1)} custom-call(f32[1,128,128]{2,1,0:T(8,128)S(1)} %get-tuple-element.36), custom_call_target="InvertDiagBlocksLowerTriangular" | custom-call | tf_op jit(solution)/shard_map/jit(cholesky)/cholesky | solution.py:36
  75.7 1.2 constant_dynamic-update-slice_fusion.3
  76.9 1.3 convolution_subtract_fusion
  78.2 11.7 %cholesky.217 = f32[128,128]{1,0:T(8,128)S(1)} custom-call(f32[128,128]{1,0:T(8,128)S(1)} %cholesky.270), custom_call_target="Cholesky" | custom-call | tf_op jit(solution)/shard_map/jit(cholesky)/cholesky | solution.py:36
  89.9 9.9 %custom-call.32 = f32[1,128,128]{1,2,0:T(8,128)S(1)} custom-call(f32[1,128,128]{2,1,0:T(8,128)S(1)} %get-tuple-element.33), custom_call_target="InvertDiagBlocksLowerTriangular" | custom-call | tf_op jit(solution)/shard_map/jit(cholesky)/cholesky | solution.py:36
  99.8 0.3 convolution_dynamic-update-slice_fusion
  100.1 1.3 convolution_subtract_fusion.1
  101.4 11.7 %cholesky.238 = f32[128,128]{1,0:T(8,128)S(1)} custom-call(f32[128,128]{1,0:T(8,128)S(1)} %cholesky.275), custom_call_target="Cholesky" | custom-call | tf_op jit(solution)/shard_map/jit(cholesky)/cholesky | solution.py:36
  113.1 0.7 compare_reduce_fusion.1
  113.9 9.8 %custom-call.33 = f32[1,128,128]{1,2,0:T(8,128)S(1)} custom-call(f32[1,128,128]{2,1,0:T(8,128)S(1)} %get-tuple-element.30), custom_call_target="InvertDiagBlocksLowerTriangular" | custom-call | tf_op jit(solution)/shard_map/jit(cholesky)/cholesky | solution.py:36
  123.9 1.2 convolution_subtract_fusion.5
  125.1 11.9 %cholesky.255 = f32[128,128]{1,0:T(8,128)S(1)} custom-call(f32[128,128]{1,0:T(8,128)S(1)} %convolution_subtract_fusion.5), custom_call_target="Cholesky" | custom-call | tf_op jit(solution)/shard_map/jit(cholesky)/cholesky | solution.py:36
  137.1 0.6 compare_reduce_fusion
  137.7 0.6 compare_reduce_fusion.2
  140.9 0.3 fusion.6
  141.2 10.4 %while.1 = (s32[]{:T(128)}, f32[512,512]{1,0:T(8,128)S(1)}, s32[4,2]{0,1:T(2,128)S(1)}, f32[4,128,128]{2,1,0:T(8,128)}, s32[]{:T(128)}) while((s32[]{:T(128)}, f32[512,512]{1,0:T(8,128)S(1)}, s32[4,2]{0,1:T(2,128)S(1)}, f32[4,128,128]{2,1,0:T(8,128)}, s32[]{:T(128)}) %tuple.35), condition=%wide.while_cond, body=%wide.while_body.sunk | while | flops 2 | bytes 132705 | solution.py:37
  141.2 0.5 fusion.58
  141.8 2.0 bitcast_dynamic-update-slice_fusion.2
  143.8 0.5 fusion.58
  144.4 2.0 bitcast_dynamic-update-slice_fusion.2
  146.4 0.5 fusion.58
  147.0 2.0 bitcast_dynamic-update-slice_fusion.2
  149.0 0.5 fusion.58
  149.6 2.0 bitcast_dynamic-update-slice_fusion.2
  151.6 40.1 %custom-call.34 = f32[4,128,128]{1,2,0:T(8,128)S(1)} custom-call(f32[4,128,128]{2,1,0:T(8,128)} %get-tuple-element.9), custom_call_target="InvertDiagBlocksLowerTriangular" | custom-call | tf_op jit(solution)/shard_map/jit(_solve_triangular)/triangular_solve | solution.py:37
  191.7 0.3 fusion.30
  192.2 0.3 fusion.29
  192.5 0.3 convolution_subtract_fusion.2
  192.8 0.3 fusion.27
  193.1 0.3 convolution_subtract_fusion.4
  193.7 0.3 fusion.26
  194.0 0.4 fusion.18
  194.5 2.6 %collective-permute-start.1 = (f32[1,128,128]{2,1,0:T(8,128)S(1)}, f32[1,128,128]{2,1,0:T(8,128)S(1)}, u32[]{:S(2)}, u32[]{:S(2)}) collective-permute-start(f32[1,128,128]{2,1,0:T(8,128)S(1)} %get-tuple-element.26), channel_id=1, source_target_pairs={{0,7},{1,0},{2,1},{3,2},{4,3},{5,4},{6,5},{7,6},{8,15},{9,8},{10,9... | collective-permute-start | bytes 196616 | tf_op jit(solution)/shard_map/ppermute | solution.py:12
  197.1 0.6 collective-permute-start.2
  197.7 2.0 collective-permute-done
  199.7 1.6 collective-permute-done.2
  201.4 0.6 fusion.35
  202.0 1.2 maximum_bitcast_fusion
  203.2 32.7 %all-reduce.3.cloned.1.call-done = f32[1,128,128]{2,1,0:T(8,128)} async-done(((f32[1,128,128]{2,1,0:T(8,128)}), f32[1,128,128]{2,1,0:T(8,128)}) %all-reduce.3.cloned.1.call-update) | async-done | bytes 65552 | tf_op jit(solution)/shard_map/psum | solution.py:86
  235.9 1.5 copy.66
  (55 shorter events, 2.6 us)
Async XLA Ops:
  9.8 10.6 %all-to-all-start = ((s32[8,1,8]{2,1,0:T(1,128)}), s32[8,1,8]{2,1,0:T(1,128)S(1)}, u32[]{:S(2)}, u32[]{:S(2)}) async-start(s32[8,1,8]{2,1,0:T(1,128)} %bitcast.6), calls=%async_computation | async-start | bytes 8192 | tf_op jit(solution)/shard_map/all_to_all | solution.py:69
  18.7 6.0 %copy-start.6 = (s32[1,8]{1,0:T(1,128)S(1)}, s32[1,8]{1,0:T(1,128)}, u32[]{:S(2)}) copy-start(s32[1,8]{1,0:T(1,128)} %param.13) | copy-start | bytes 100
  18.7 6.0 %copy-start.7 = (s32[1,8]{1,0:T(1,128)S(1)}, s32[1,8]{1,0:T(1,128)}, u32[]{:S(2)}) copy-start(s32[1,8]{1,0:T(1,128)} %param.12) | copy-start | bytes 100
  18.7 7.3 %copy-start.8 = (s32[50]{0:T(128)S(1)}, s32[50]{0:T(128)}, u32[]{:S(2)}) copy-start(s32[50]{0:T(128)} %constant.222) | copy-start | bytes 604
  18.7 7.3 %copy-start.4 = (f32[1,8,640]{2,1,0:T(8,128)S(1)}, f32[1,8,640]{2,1,0:T(8,128)}, u32[]{:S(2)}) copy-start(f32[1,8,640]{2,1,0:T(8,128)} %param.14) | copy-start | bytes 61444
  20.4 19.6 %all-to-all-start.1 = ((bf16[8,8,64,128]{3,1,2,0:T(8,128)(2,1)}), bf16[8,8,64,128]{3,1,2,0:T(8,128)(2,1)S(1)}, u32[]{:S(2)}, u32[]{:S(2)}) async-start(bf16[8,8,64,128]{3,1,2,0:T(8,128)(2,1)} %copy.28), calls=%async_computation.1 | async-start | bytes 2097152 | tf_op jit(solution)/shard_map/all_to_all | solution.py:62
  24.6 211.2 %all-reduce.3.cloned.1.call-start = ((), (), s32[]{:S(2)}) async-start(), calls=%async_computation.2 | async-start | bytes 131072 | tf_op jit(solution)/shard_map/psum | solution.py:86
  40.9 0.7 copy-start.5
  47.0 2.0 copy-start
  49.5 1.5 copy-start.1
  51.1 1.7 copy-start.2
  53.0 1.0 copy-start.3
  194.4 5.3 %collective-permute-start = (f32[1,128,128]{2,1,0:T(8,128)S(1)}, f32[1,128,128]{2,1,0:T(8,128)S(1)}, u32[]{:S(2)}, u32[]{:S(2)}) collective-permute-start(f32[1,128,128]{2,1,0:T(8,128)S(1)} %get-tuple-element.24), channel_id=1, source_target_pairs={{0,1},{1,2},{2,3},{3,4},{4,5},{5,6},{6,7},{7,0},{8,9},{9,10},{10,1... | collective-permute-start | bytes 196616 | tf_op jit(solution)/shard_map/ppermute | solution.py:12
  194.5 5.3 %collective-permute-start.1 = (f32[1,128,128]{2,1,0:T(8,128)S(1)}, f32[1,128,128]{2,1,0:T(8,128)S(1)}, u32[]{:S(2)}, u32[]{:S(2)}) collective-permute-start(f32[1,128,128]{2,1,0:T(8,128)S(1)} %get-tuple-element.26), channel_id=1, source_target_pairs={{0,7},{1,0},{2,1},{3,2},{4,3},{5,4},{6,5},{7,6},{8,15},{9,8},{10,9... | collective-permute-start | bytes 196616 | tf_op jit(solution)/shard_map/ppermute | solution.py:12
  197.1 4.3 %collective-permute-start.2 = (f32[1,128,128]{2,1,0:T(8,128)S(1)}, f32[1,128,128]{2,1,0:T(8,128)S(1)}, u32[]{:S(2)}, u32[]{:S(2)}) collective-permute-start(f32[1,128,128]{2,1,0:T(8,128)S(1)} %get-tuple-element.25), channel_id=1, source_target_pairs={{0,4},{1,5},{2,6},{3,7},{4,0},{5,1},{6,2},{7,3},{8,12},{9,13},{10,... | collective-permute-start | bytes 196616 | tf_op jit(solution)/shard_map/ppermute | solution.py:12
Sparse Core Ops, SparseCore 0:
  202.1 33.6 all-reduce.2
where the time goes:
time: 245 us; the launch traced here: 244 us
  other arithmetic  126 us (51%)
  waiting for transfers between devices  49 us (20%)
  local copies, waits for them, and re-layouts  30.5 us (12%)
  between operations  17.7 us (7%)
  starting transfers between devices  12.7 us (5%)
  matrix products  8.06 us (3%)
    another operation x14, other arithmetic, front_factor(): jnp.linalg.cholesky(front_matrix[:elimination_count, :elimination_count])  78.7 us
    another operation x3, other arithmetic, front_factor(): jax.scipy.linalg.solve_triangular(lower_triangle, front_matrix[eliminatio...  40.4 us
    psum x1, waiting for transfers between devices, body(): total = lax.psum(local_sum, 'grp')  32.7 us
    all_to_all x1, waiting for transfers between devices, body(): lax.all_to_all(outgoing.reshape(width, room, rows, column_indices), 'sep'...  12.6 us
    another operation x12, local copies, waits for them, and re-layouts  10.4 us
    another operation x6, matrix products, front_factor(): jnp.linalg.cholesky(front_matrix[:elimination_count, :elimination_count])  5.47 us
    all_to_all x1, starting transfers between devices, body(): lax.all_to_all(labels.reshape(width, room), 'sep', split_axis=0, concat_a...  5.2 us
  transfers between devices with their start and end apart: 6, of which 4 were waited for; matrix products, arithmetic and copies ran while one was open for 3% of the time, Pallas kernels for 0%

commit v1 on v0

--- a/solution.py
+++ b/solution.py
@@ -83,7 +83,7 @@
     for offset in (1, -1, width // 2):
         piece = jnp.where(distance == offset % width, schur, 0.0)[None]
         local_sum = local_sum + passed_along(piece, "sep", offset)
-    total = lax.psum(local_sum, "grp")
+    total = jnp.sum(lax.all_gather(local_sum, "grp"), axis=0)
     return (factor[None, None], total)
 
 

time: 245 us -> 211 us (0.86)
  waiting for transfers between devices: 49 us -> 15.2 us
  blocking collectives: 0 us -> 14.7 us
  between operations: 17.7 us -> 4.32 us
    psum x1 -> x0, waiting for transfers between devices: 32.7 us -> none  [body(): total = lax.psum(local_sum, 'grp')]
    all_gather x0 -> x1, blocking collectives: none -> 14.7 us  [body(): total = jnp.sum(lax.all_gather(local_sum, 'grp'), axis=0)]
  transfers between devices with their start and end apart: 6 -> 5, of which waited for: 4 -> 3; matrix products, arithmetic and copies ran while one was open for 3% -> 4% of each run, Pallas kernels for 0% -> 0%
where the time goes in v1:
time: 211 us; the launch traced here: 210 us
  other arithmetic  126 us (60%)
  local copies, waits for them, and re-layouts  29 us (14%)
  waiting for transfers between devices  15.2 us (7%)
  blocking collectives  14.7 us (7%)
  starting transfers between devices  12.6 us (6%)
  matrix products  8.07 us (4%)
  between operations  4.32 us (2%)
    another operation x14, other arithmetic, front_factor(): jnp.linalg.cholesky(front_matrix[:elimination_count, :elimination_count])  78.7 us
    another operation x3, other arithmetic, front_factor(): jax.scipy.linalg.solve_triangular(lower_triangle, front_matrix[eliminatio...  40.4 us
    all_gather x1, blocking collectives, body(): total = jnp.sum(lax.all_gather(local_sum, 'grp'), axis=0)  14.7 us
    all_to_all x1, waiting for transfers between devices, body(): lax.all_to_all(outgoing.reshape(width, room, rows, column_indices), 'sep'...  12.7 us
    another operation x12, local copies, waits for them, and re-layouts  10.4 us
    another operation x6, matrix products, front_factor(): jnp.linalg.cholesky(front_matrix[:elimination_count, :elimination_count])  5.47 us
    all_to_all x1, starting transfers between devices, body(): lax.all_to_all(labels.reshape(width, room), 'sep', split_axis=0, concat_a...  5.2 us
  transfers between devices with their start and end apart: 5, of which 3 were waited for; matrix products, arithmetic and copies ran while one was open for 4% of the time, Pallas kernels for 0%

profile of v1, /device:TPU:0, one launch (start us, length us, event | category | flops | bytes accessed | tf_op | source)
XLA Modules:
  0.0 210.2 jit_solution(14879314507736936798)
XLA Ops:
  0.6 0.9 select_reduce_fusion.5
  1.8 0.8 scatter_custom_fusion
  2.6 0.7 all_to_all.9
  3.3 5.2 %all-to-all-start = ((s32[8,1,8]{2,1,0:T(1,128)}), s32[8,1,8]{2,1,0:T(1,128)S(1)}, u32[]{:S(2)}, u32[]{:S(2)}) async-start(s32[8,1,8]{2,1,0:T(1,128)} %bitcast.6), calls=%async_computation | async-start | bytes 8192 | tf_op jit(solution)/shard_map/all_to_all | solution.py:69
  8.5 0.2 broadcast_in_dim.90
  8.7 3.4 %scatter_fusion = bf16[64,64,128]{2,1,0:T(8,128)(2,1)S(1)} fusion(bf16[64,64,128]{2,1,0:T(8,128)(2,1)S(1)} %broadcast_in_dim.90, s32[32]{0:T(128)S(1)} %fusion.44, bf16[32,64,128]{2,1,0:T(8,128)(2,1)} %bitcast.121), kind=kCustom, calls=%fused_computation.2 | custom fusion | bytes 1572992 | tf_op jit(solution)/shard_map/scatter | solution.py:59
  12.2 1.7 copy.28
  13.9 4.2 %all-to-all-start.1 = ((bf16[8,8,64,128]{3,1,2,0:T(8,128)(2,1)}), bf16[8,8,64,128]{3,1,2,0:T(8,128)(2,1)S(1)}, u32[]{:S(2)}, u32[]{:S(2)}) async-start(bf16[8,8,64,128]{3,1,2,0:T(8,128)(2,1)} %copy.28), calls=%async_computation.1 | async-start | bytes 2097152 | tf_op jit(solution)/shard_map/all_to_all | solution.py:62
  18.1 0.6 fusion.45
  19.5 0.5 broadcast.253
  20.0 0.7 reduce.30
  20.8 12.7 %all-to-all-done.1 = bf16[8,8,64,128]{3,1,2,0:T(8,128)(2,1)S(1)} async-done(((bf16[8,8,64,128]{3,1,2,0:T(8,128)(2,1)}), bf16[8,8,64,128]{3,1,2,0:T(8,128)(2,1)S(1)}, u32[]{:S(2)}, u32[]{:S(2)}) %all-to-all-start.1) | async-done | bytes 1048608 | tf_op jit(solution)/shard_map/all_to_all | solution.py:62
  33.4 0.3 fusion.3
  33.7 0.6 copy.30
  34.3 0.7 gather_fusion
  35.2 1.0 copy.31
  36.2 1.6 copy.49
  37.8 2.7 %copy.32 = f32[640,640]{0,1:T(8,128)} copy(f32[640,640]{1,0:T(8,128)} %bitcast.119) | data formatting | bytes 3276800 | tf_op jit(solution)/shard_map/reshape | solution.py:33
  40.5 2.0 fusion.7
  42.5 0.5 select_subtract_fusion
  43.0 1.2 slice.135
  44.2 0.3 copy-done.1
  44.6 1.7 copy.33
  46.5 1.0 copy-done.3
  47.4 11.7 %cholesky.104 = f32[128,128]{1,0:T(8,128)S(1)} custom-call(f32[128,128]{1,0:T(8,128)S(1)} %cholesky.266), custom_call_target="Cholesky" | custom-call | tf_op jit(solution)/shard_map/jit(cholesky)/cholesky | solution.py:36
  59.2 9.8 %custom-call.31 = f32[1,128,128]{1,2,0:T(8,128)S(1)} custom-call(f32[1,128,128]{2,1,0:T(8,128)S(1)} %get-tuple-element.36), custom_call_target="InvertDiagBlocksLowerTriangular" | custom-call | tf_op jit(solution)/shard_map/jit(cholesky)/cholesky | solution.py:36
  69.1 1.2 constant_dynamic-update-slice_fusion.3
  70.4 1.3 convolution_subtract_fusion
  71.6 11.7 %cholesky.217 = f32[128,128]{1,0:T(8,128)S(1)} custom-call(f32[128,128]{1,0:T(8,128)S(1)} %cholesky.270), custom_call_target="Cholesky" | custom-call | tf_op jit(solution)/shard_map/jit(cholesky)/cholesky | solution.py:36
  83.4 9.9 %custom-call.32 = f32[1,128,128]{1,2,0:T(8,128)S(1)} custom-call(f32[1,128,128]{2,1,0:T(8,128)S(1)} %get-tuple-element.33), custom_call_target="InvertDiagBlocksLowerTriangular" | custom-call | tf_op jit(solution)/shard_map/jit(cholesky)/cholesky | solution.py:36
  93.3 0.3 convolution_dynamic-update-slice_fusion
  93.6 1.3 convolution_subtract_fusion.1
  94.9 11.7 %cholesky.238 = f32[128,128]{1,0:T(8,128)S(1)} custom-call(f32[128,128]{1,0:T(8,128)S(1)} %cholesky.275), custom_call_target="Cholesky" | custom-call | tf_op jit(solution)/shard_map/jit(cholesky)/cholesky | solution.py:36
  106.6 0.7 compare_reduce_fusion.1
  107.3 9.8 %custom-call.33 = f32[1,128,128]{1,2,0:T(8,128)S(1)} custom-call(f32[1,128,128]{2,1,0:T(8,128)S(1)} %get-tuple-element.30), custom_call_target="InvertDiagBlocksLowerTriangular" | custom-call | tf_op jit(solution)/shard_map/jit(cholesky)/cholesky | solution.py:36
  117.4 1.2 convolution_subtract_fusion.5
  118.6 11.9 %cholesky.255 = f32[128,128]{1,0:T(8,128)S(1)} custom-call(f32[128,128]{1,0:T(8,128)S(1)} %convolution_subtract_fusion.5), custom_call_target="Cholesky" | custom-call | tf_op jit(solution)/shard_map/jit(cholesky)/cholesky | solution.py:36
  130.5 0.6 compare_reduce_fusion
  131.2 0.6 compare_reduce_fusion.2
  134.4 0.3 fusion.6
  134.6 10.4 %while.1 = (s32[]{:T(128)}, f32[512,512]{1,0:T(8,128)S(1)}, s32[4,2]{0,1:T(2,128)S(1)}, f32[4,128,128]{2,1,0:T(8,128)}, s32[]{:T(128)}) while((s32[]{:T(128)}, f32[512,512]{1,0:T(8,128)S(1)}, s32[4,2]{0,1:T(2,128)S(1)}, f32[4,128,128]{2,1,0:T(8,128)}, s32[]{:T(128)}) %tuple.35), condition=%wide.while_cond, body=%wide.while_body.sunk | while | flops 2 | bytes 132705 | solution.py:37
  134.7 0.5 fusion.58
  135.2 2.0 bitcast_dynamic-update-slice_fusion.2
  137.3 0.5 fusion.58
  137.8 2.0 bitcast_dynamic-update-slice_fusion.2
  139.9 0.5 fusion.58
  140.4 2.0 bitcast_dynamic-update-slice_fusion.2
  142.5 0.5 fusion.58
  143.0 2.0 bitcast_dynamic-update-slice_fusion.2
  145.0 40.1 %custom-call.34 = f32[4,128,128]{1,2,0:T(8,128)S(1)} custom-call(f32[4,128,128]{2,1,0:T(8,128)} %get-tuple-element.9), custom_call_target="InvertDiagBlocksLowerTriangular" | custom-call | tf_op jit(solution)/shard_map/jit(_solve_triangular)/triangular_solve | solution.py:37
  185.2 0.3 fusion.30
  185.7 0.3 fusion.29
  186.0 0.3 convolution_subtract_fusion.2
  186.2 0.3 fusion.27
  186.5 0.3 convolution_subtract_fusion.4
  187.1 0.3 fusion.26
  187.4 0.4 fusion.18
  188.0 2.6 %collective-permute-start.1 = (f32[1,128,128]{2,1,0:T(8,128)S(1)}, f32[1,128,128]{2,1,0:T(8,128)S(1)}, u32[]{:S(2)}, u32[]{:S(2)}) collective-permute-start(f32[1,128,128]{2,1,0:T(8,128)S(1)} %get-tuple-element.26), channel_id=1, source_target_pairs={{0,7},{1,0},{2,1},{3,2},{4,3},{5,4},{6,5},{7,6},{8,15},{9,8},{10,9... | collective-permute-start | bytes 196616 | tf_op jit(solution)/shard_map/ppermute | solution.py:12
  190.6 0.6 collective-permute-start.2
  191.1 1.1 maximum_bitcast_fusion
  192.3 0.9 collective-permute-done
  193.2 1.6 collective-permute-done.2
  194.9 14.7 %all-gather = f32[4,128,128]{2,1,0:T(8,128)S(1)} all-gather(f32[1,128,128]{2,1,0:T(8,128)S(1)} %fusion.35), channel_id=2, replica_groups=mesh['grp'=4,'sep'=8] {'grp'}, dimensions={0}, use_global_device_ids=true | all-gather | bytes 327680 | tf_op jit(solution)/shard_map/all_gather | solution.py:86
  209.6 0.6 reduce.25
  (53 shorter events, 2.3 us)
Async XLA Ops:
  3.3 10.6 %all-to-all-start = ((s32[8,1,8]{2,1,0:T(1,128)}), s32[8,1,8]{2,1,0:T(1,128)S(1)}, u32[]{:S(2)}, u32[]{:S(2)}) async-start(s32[8,1,8]{2,1,0:T(1,128)} %bitcast.6), calls=%async_computation | async-start | bytes 8192 | tf_op jit(solution)/shard_map/all_to_all | solution.py:69
  12.1 6.0 %copy-start.6 = (s32[1,8]{1,0:T(1,128)S(1)}, s32[1,8]{1,0:T(1,128)}, u32[]{:S(2)}) copy-start(s32[1,8]{1,0:T(1,128)} %param.13) | copy-start | bytes 100
  12.1 5.9 %copy-start.7 = (s32[1,8]{1,0:T(1,128)S(1)}, s32[1,8]{1,0:T(1,128)}, u32[]{:S(2)}) copy-start(s32[1,8]{1,0:T(1,128)} %param.12) | copy-start | bytes 100
  12.1 7.3 %copy-start.8 = (s32[50]{0:T(128)S(1)}, s32[50]{0:T(128)}, u32[]{:S(2)}) copy-start(s32[50]{0:T(128)} %constant.222) | copy-start | bytes 604
  12.2 7.3 %copy-start.4 = (f32[1,8,640]{2,1,0:T(8,128)S(1)}, f32[1,8,640]{2,1,0:T(8,128)}, u32[]{:S(2)}) copy-start(f32[1,8,640]{2,1,0:T(8,128)} %param.14) | copy-start | bytes 61444
  13.9 19.6 %all-to-all-start.1 = ((bf16[8,8,64,128]{3,1,2,0:T(8,128)(2,1)}), bf16[8,8,64,128]{3,1,2,0:T(8,128)(2,1)S(1)}, u32[]{:S(2)}, u32[]{:S(2)}) async-start(bf16[8,8,64,128]{3,1,2,0:T(8,128)(2,1)} %copy.28), calls=%async_computation.1 | async-start | bytes 2097152 | tf_op jit(solution)/shard_map/all_to_all | solution.py:62
  34.3 0.7 copy-start.5
  40.5 2.0 copy-start
  43.0 1.5 copy-start.1
  44.5 1.7 copy-start.2
  46.4 1.0 copy-start.3
  187.9 5.3 %collective-permute-start = (f32[1,128,128]{2,1,0:T(8,128)S(1)}, f32[1,128,128]{2,1,0:T(8,128)S(1)}, u32[]{:S(2)}, u32[]{:S(2)}) collective-permute-start(f32[1,128,128]{2,1,0:T(8,128)S(1)} %get-tuple-element.24), channel_id=1, source_target_pairs={{0,1},{1,2},{2,3},{3,4},{4,5},{5,6},{6,7},{7,0},{8,9},{9,10},{10,1... | collective-permute-start | bytes 196616 | tf_op jit(solution)/shard_map/ppermute | solution.py:12
  188.0 5.3 %collective-permute-start.1 = (f32[1,128,128]{2,1,0:T(8,128)S(1)}, f32[1,128,128]{2,1,0:T(8,128)S(1)}, u32[]{:S(2)}, u32[]{:S(2)}) collective-permute-start(f32[1,128,128]{2,1,0:T(8,128)S(1)} %get-tuple-element.26), channel_id=1, source_target_pairs={{0,7},{1,0},{2,1},{3,2},{4,3},{5,4},{6,5},{7,6},{8,15},{9,8},{10,9... | collective-permute-start | bytes 196616 | tf_op jit(solution)/shard_map/ppermute | solution.py:12
  190.6 4.3 %collective-permute-start.2 = (f32[1,128,128]{2,1,0:T(8,128)S(1)}, f32[1,128,128]{2,1,0:T(8,128)S(1)}, u32[]{:S(2)}, u32[]{:S(2)}) collective-permute-start(f32[1,128,128]{2,1,0:T(8,128)S(1)} %get-tuple-element.25), channel_id=1, source_target_pairs={{0,4},{1,5},{2,6},{3,7},{4,0},{5,1},{6,2},{7,3},{8,12},{9,13},{10,... | collective-permute-start | bytes 196616 | tf_op jit(solution)/shard_map/ppermute | solution.py:12
